TPU v7x, 256 devices: a whole 4x4x8 slice. The times are simulated.
256 devices in a mesh: gx: 32 (over z, x_hi, core), gy: 8 (over x_lo, y).
Axes of the slice: x: 4 (x_hi: 2, x_lo: 2; x = x_hi * 2 + x_lo), y: 4, z: 8, core: 2. Of those that a mesh axis runs over, the one named last changes fastest.
Arguments:
- conc: float32 [32, 2048, 1024], P(None, 'gx', 'gy'), may hold values from -4 to 4
- mobility: float32 [32, 2048, 1024], P(None, 'gx', 'gy'), may hold values from 0.3 to 3
- block_x: float32 [32, 2048, 64], P(None, 'gx'), may hold values from -0.75 to 0.75
- spike_x: float32 [32, 2048, 4], P(None, 'gx'), may hold values from -3 to 3
- reduced_x: float32 [32, 128, 128], replicated, may hold values from -0.5 to 0.5
- block_y: float32 [32, 1024, 128], P(None, 'gy'), may hold values from -0.5 to 0.5
- spike_y: float32 [32, 1024, 4], P(None, 'gy'), may hold values from -3 to 3
- reduced_y: float32 [32, 32, 32], replicated, may hold values from -1 to 1
Outputs:
- conc_next: float32 [32, 2048, 1024], P(None, 'gx', 'gy')
All inputs are finite; a program needn't handle non-finite values.
Results may differ from a plain program's by a relative error of at most 0.00012.
Values sent between devices are 32-bit elements; how exact they have to be, the bound alone decides.
No kernel may reach another device: no remote copies, remote signals or barrier semaphores. Data moves between devices by JAX's collectives and lax.ppermute only.
A program may use at most 64 MiB of HBM per device.

v0:
```python
import jax
import jax.numpy as jnp
from jax import lax
from jax.sharding import PartitionSpec as P

HIGH = lax.Precision.HIGHEST


def extended_2(shard, sides, width):
    for axis, dim in sides:
        devices, length = (lax.axis_size(axis), shard.shape[dim])
        up = [(i, (i + 1) % devices) for i in range(devices)]
        down = [(j, i) for i, j in up]
        last = lax.slice_in_dim(shard, length - width, length, axis=dim)
        leading = lax.slice_in_dim(shard, 0, width, axis=dim)
        before = lax.ppermute(last, axis, up)
        after = lax.ppermute(leading, axis, down)
        shard = jnp.concatenate([before, shard, after], axis=dim)
    return shard


def divergence(conc, mu_ext, mob_ext):
    mu_mid = mu_ext[:, 1:-1, 1:-1]
    mob_mid = mob_ext[:, 1:-1, 1:-1]
    total = jnp.zeros_like(conc)
    for lo_x, hi_x, lo_y, hi_y in (
        (2, None, 1, -1),
        (0, -2, 1, -1),
        (1, -1, 2, None),
        (1, -1, 0, -2),
    ):
        mu_side = mu_ext[:, lo_x:hi_x, lo_y:hi_y]
        mob_side = mob_ext[:, lo_x:hi_x, lo_y:hi_y]
        total = total + 0.5 * (mob_side + mob_mid) * (mu_side - mu_mid)
    return conc + 0.02 * total


def laplace(padded):
    return (
        padded[:, 2:, 1:-1]
        + padded[:, :-2, 1:-1]
        + padded[:, 1:-1, 2:]
        + padded[:, 1:-1, :-2]
        - 4.0 * padded[:, 1:-1, 1:-1]
    )


def potential(centre, lap):
    return centre * centre * centre - centre - 1.0 * lap


def mobile(prefactor, centre):
    sq = centre * centre
    return prefactor * (0.25 + sq) / (1.0 + sq)


def solve_x(field, block_x, spike_x, reduced_x):
    width = field.shape[1]
    lin = jnp.einsum("zij,zjn->zin", block_x, field, precision=HIGH)
    rims = jnp.concatenate([lin[:, 0:2], lin[:, width - 2 :]], axis=1)
    whole = reduced_x.shape[1]
    place = lax.axis_index("gx")
    gathered = lax.all_gather(rims, "gx", axis=1, tiled=True)
    offsets = jnp.array([-2, -1, 4, 5], jnp.int32)
    picks = (4 * place + offsets) % whole
    rows_used = jnp.take(reduced_x, picks, axis=1)
    coupled = jnp.einsum("zrk,zkn->zrn", rows_used, gathered, precision=HIGH)
    return lin - jnp.einsum("zik,zkn->zin", spike_x, coupled, precision=HIGH)


def solve_y(field, block_y, spike_y, reduced_y):
    width = field.shape[2]
    lin = jnp.einsum("zij,zxj->zxi", block_y, field, precision=HIGH)
    rims = jnp.transpose(
        jnp.concatenate([lin[:, :, 0:2], lin[:, :, width - 2 :]], axis=2), (0, 2, 1)
    )
    gathered = lax.all_gather(rims, "gy", axis=1, tiled=True)
    whole = reduced_y.shape[1]
    place = lax.axis_index("gy")
    offsets = jnp.array([-2, -1, 4, 5], jnp.int32)
    picks = (4 * place + offsets) % whole
    rows_used = jnp.take(reduced_y, picks, axis=1)
    coupled = jnp.einsum("zrk,zkx->zrx", rows_used, gathered, precision=HIGH)
    return lin - jnp.einsum("zik,zkx->zxi", spike_y, coupled, precision=HIGH)


def body(conc, mobility, block_x, spike_x, reduced_x, block_y, spike_y, reduced_y):
    padded = extended_2(conc, (("gx", 1), ("gy", 2)), 1)
    mu_here = potential(conc, laplace(padded))
    mob_here = mobile(mobility, conc)
    extended = extended_2(jnp.stack([mu_here, mob_here]), (("gx", 2), ("gy", 3)), 1)
    rhs = divergence(conc, extended[0], extended[1])
    xsol = solve_x(rhs, block_x, spike_x, reduced_x)
    return solve_y(xsol, block_y, spike_y, reduced_y)


def solution(mesh):
    in_specs = (
        P(None, "gx", "gy"),
        P(None, "gx", "gy"),
        P(None, "gx", None),
        P(None, "gx", None),
        P(),
        P(None, "gy", None),
        P(None, "gy", None),
        P(),
    )
    out_specs = P(None, "gx", "gy")
    return jax.shard_map(body, mesh=mesh, in_specs=in_specs, out_specs=out_specs, check_vma=False)
```

profile of v0, /device:TPU:24, one launch (start us, length us, event | category | flops | bytes accessed | tf_op | source)
XLA Modules:
  0.0 214.3 jit_solution(208142378381438117)
XLA Ops:
  7.7 7.8 %collective-permute-start = (f32[32,1,128]{2,0,1:T(8,128)S(1)}, f32[32,1,128]{2,0,1:T(8,128)S(1)}, u32[]{:S(2)}, u32[]{:S(2)}) collective-permute-start(f32[32,1,128]{2,0,1:T(8,128)S(1)} %bitcast.50), channel_id=1, source_target_pairs={{8,0},{16,8},{24,16},{32,24},{40,32},{48,40},{56,48},{64,56},{72,6... | collective-permute-start | bytes 49160 | tf_op jit(solution)/shard_map/ppermute | solution.py:17
  15.5 1.4 collective-permute-done
  17.0 5.3 %collective-permute-done.1 = f32[32,1,128]{2,0,1:T(8,128)S(1)} collective-permute-done((f32[32,1,128]{2,0,1:T(8,128)S(1)}, f32[32,1,128]{2,0,1:T(8,128)S(1)}, u32[]{:S(2)}, u32[]{:S(2)}) %collective-permute-start.1) | collective-permute-done | bytes 16416 | tf_op jit(solution)/shard_map/ppermute | solution.py:16
  22.3 1.3 pad_maximum_fusion.2
  23.6 1.4 fusion.54
  25.1 1.7 copy.61
  28.0 3.4 %collective-permute-start.3 = (f32[32,66,1]{1,0,2:T(8,128)S(1)}, f32[32,66,1]{1,0,2:T(8,128)S(1)}, u32[]{:S(2)}, u32[]{:S(2)}) collective-permute-start(f32[32,66,1]{1,0,2:T(8,128)S(1)} %copy.63), channel_id=1, source_target_pairs={{0,1},{1,2},{2,3},{3,4},{4,5},{5,6},{6,7},{7,0},{8,9},{9,10},{10,1... | collective-permute-start | bytes 25352 | tf_op jit(solution)/shard_map/ppermute | solution.py:16
  32.6 1.5 copy.62
  34.2 1.5 copy.64
  35.7 5.3 %fusion.7 = (f32[1,32,64,128]{3,2,1,0:T(8,128)S(1)}, f32[1,32,64,128]{3,2,1,0:T(8,128)S(1)}) fusion(f32[32,64,128]{2,1,0:T(8,128)} %param.10, f32[32,66,1]{2,1,0:T(8,128)} %copy.64, f32[32,1,128]{2,1,0:T(1,128)S(1)} %bitcast.44, f32[32,1,128]{2,1,0:T(1,128)S(1)} %bitcast.46, f32[32,66,1]{2,1,0:T(8,128)} %copy.62, f32[32,64,128]{2,1,0:T(8,128)} %param.11), kind=kLoop, calls=%fused_computation.20 | loop fusion | flops 5505024 | bytes 4243968 | tf_op jit(solution)/shard_map/stack | solution.py:91
  41.2 5.3 %collective-permute-start.5 = (f32[2,32,1,128]{3,1,2,0:T(8,128)S(1)}, f32[2,32,1,128]{3,1,2,0:T(8,128)S(1)}, u32[]{:S(2)}, u32[]{:S(2)}) collective-permute-start(f32[2,32,1,128]{3,1,2,0:T(8,128)S(1)} %bitcast.47), channel_id=1, source_target_pairs={{8,0},{16,8},{24,16},{32,24},{40,32},{48,40},{56,48},{64,56},{72,6... | collective-permute-start | bytes 98312 | tf_op jit(solution)/shard_map/ppermute | solution.py:17
  46.5 1.6 collective-permute-done.4
  48.5 2.9 %fusion.53 = (f32[2,32,66,1]{3,2,1,0:T(8,128)}, f32[2,32,66,1]{3,2,1,0:T(8,128)}) fusion(f32[2,32,66,128]{3,2,1,0:T(8,128)S(1)} %pad_maximum_fusion.1), kind=kLoop, calls=%fused_computation.90 | loop fusion | bytes 67584 | tf_op jit(solution)/shard_map/slice | solution.py:14
  51.4 2.4 %copy.69 = f32[2,32,66,1]{2,1,3,0:T(8,128)S(1)} copy(f32[2,32,66,1]{3,2,1,0:T(8,128)} %get-tuple-element.11) | data formatting | bytes 33792 | tf_op jit(solution)/shard_map/slice | solution.py:14
  53.8 3.2 %collective-permute-start.6 = (f32[2,32,66,1]{2,1,3,0:T(8,128)S(1)}, f32[2,32,66,1]{2,1,3,0:T(8,128)S(1)}, u32[]{:S(2)}, u32[]{:S(2)}) collective-permute-start(f32[2,32,66,1]{2,1,3,0:T(8,128)S(1)} %copy.69), channel_id=1, source_target_pairs={{0,1},{1,2},{2,3},{3,4},{4,5},{5,6},{6,7},{7,0},{8,9},{9,10},{10,1... | collective-permute-start | bytes 50696 | tf_op jit(solution)/shard_map/ppermute | solution.py:16
  57.0 2.4 %copy.70 = f32[2,32,66,1]{2,1,3,0:T(8,128)S(1)} copy(f32[2,32,66,1]{3,2,1,0:T(8,128)} %get-tuple-element.12) | data formatting | bytes 33792 | tf_op jit(solution)/shard_map/slice | solution.py:15
  59.7 2.3 %copy.71 = f32[2,32,66,1]{3,2,1,0:T(8,128)} copy(f32[2,32,66,1]{2,1,3,0:T(8,128)S(1)} %collective-permute-done.6) | data formatting | bytes 33792 | tf_op jit(solution)/shard_map/ppermute | solution.py:16
  62.0 3.7 %collective-permute-done.7 = f32[2,32,66,1]{2,1,3,0:T(8,128)S(1)} collective-permute-done((f32[2,32,66,1]{2,1,3,0:T(8,128)S(1)}, f32[2,32,66,1]{2,1,3,0:T(8,128)S(1)}, u32[]{:S(2)}, u32[]{:S(2)}) %collective-permute-start.7) | collective-permute-done | bytes 16928 | tf_op jit(solution)/shard_map/ppermute | solution.py:17
  65.7 2.3 %copy.72 = f32[2,32,66,1]{3,2,1,0:T(8,128)} copy(f32[2,32,66,1]{2,1,3,0:T(8,128)S(1)} %collective-permute-done.7) | data formatting | bytes 33792 | tf_op jit(solution)/shard_map/ppermute | solution.py:17
  68.0 5.2 %pad_maximum_fusion = f32[2,32,66,130]{3,2,1,0:T(8,128)S(1)} fusion(f32[2,32,66,1]{3,2,1,0:T(8,128)} %copy.72, f32[2,32,1,128]{3,2,1,0:T(1,128)S(1)} %bitcast.42, f32[1,32,64,128]{3,2,1,0:T(8,128)} %copy-done.1, f32[1,32,64,128]{3,2,1,0:T(8,128)S(1)} %get-tuple-element.21, f32[2,32,1,128]{3,2,1,0:T(1,128)S(1)} %bitcast.40, f32[2,32,66,1]{3,2,1,0:T(8,128)} %copy.71), kind=kLoop, calls=%fused_computation.2 | loop fusion | flops 2745600 | bytes 4392960 | tf_op jit(solution)/shard_map/concatenate | solution.py:18
  74.4 5.3 %convolution_bitcast_fusion.1 = f32[32,64,128]{2,1,0:T(8,128)} fusion(f32[32,64,64]{2,1,0:T(8,128)} %param.12, f32[32,64,128]{2,1,0:T(8,128)S(1)} %copy-done.2, f32[32,66,130]{2,1,0:T(8,128)S(1)} %get-tuple-element.10, f32[32,66,130]{2,1,0:T(8,128)S(1)} %get-tuple-element.9), kind=kOutput, calls=%fused_computation.14 | convolution fusion | flops 206831616 | bytes 13107200 | tf_op jit(solution)/shard_map/zij,zjn->zin/dot_general | solution.py:59
  81.6 1.6 gather_fusion
  83.2 1.7 gather_fusion.1
  84.9 74.2 %all-gather.2.cloned.1.call-done = f32[32,128,128]{2,0,1:T(8,128)} async-done(((f32[32,4,128]{2,0,1:T(8,128)}), f32[32,128,128]{2,0,1:T(8,128)}) %all-gather.2.cloned.1.call-update) | async-done | bytes 2097168 | tf_op jit(solution)/shard_map/all_gather | solution.py:63
  159.1 4.4 %fusion = f32[32,4,128]{2,1,0:T(4,128)S(1)} fusion(f32[32,128,128]{2,0,1:T(8,128)} %all-gather.2.cloned.1.call-done, f32[4,32,128]{2,0,1:T(4,128)S(1)} %gather_fusion, pred[4]{0:T(512)(128)(4,1)S(1)} %get-tuple-element.25), kind=kOutput, calls=%fused_computation.6 | convolution fusion | flops 25182208 | bytes 2228228 | tf_op jit(solution)/shard_map/zrk,zkn->zrn/dot_general | solution.py:67
  163.4 1.8 fusion.2
  165.3 4.1 %fusion.58 = f32[32,64,128]{2,1,0:T(8,128)S(1)} fusion(f32[32,64,128]{2,1,0:T(8,128)S(1)} %fusion.2, f32[32,128,128]{2,1,0:T(8,128)S(1)} %copy-done), kind=kOutput, calls=%fused_computation.95 | convolution fusion | flops 402653184 | bytes 4194304 | tf_op jit(solution)/shard_map/zij,zxj->zxi/dot_general | solution.py:73
  169.4 1.7 fusion.55
  171.2 1.6 copy.75
  172.8 1.6 copy.76
  174.4 29.4 %all_gather.7 = f32[32,32,64]{2,0,1:T(8,128)S(1)} all-gather(f32[32,4,64]{2,0,1:T(8,128)S(1)} %maximum_bitcast_fusion), channel_id=1, replica_groups=mesh['gx'=32,'gy'=8] {'gy'}, dimensions={1}, use_global_device_ids=true | all-gather | bytes 294912 | tf_op jit(solution)/shard_map/all_gather | solution.py:77
  204.6 2.8 %convolution_subtract_fusion = f32[32,64,128]{2,1,0:T(8,128)} fusion(f32[32,64,128]{2,1,0:T(8,128)S(1)} %fusion.58, f32[32,4,64]{2,1,0:T(4,128)S(1)} %fusion.35, f32[32,128,4]{1,2,0:T(4,128)S(1)} %copy-done.5), kind=kOutput, calls=%fused_computation.11 | convolution fusion | flops 12845056 | bytes 2195456 | tf_op jit(solution)/shard_map/zik,zkx->zxi/dot_general | solution.py:84
  (37 shorter events, 8.2 us)
Async XLA Ops:
  6.5 158.7 %copy-start = (f32[32,128,128]{2,1,0:T(8,128)S(1)}, f32[32,128,128]{2,1,0:T(8,128)}, u32[]{:S(2)}) copy-start(f32[32,128,128]{2,1,0:T(8,128)} %param.15) | copy-start | bytes 6291460
  6.5 152.5 %all-gather.2.cloned.1.call-start = ((), (), s32[]{:S(2)}) async-start(), calls=%async_computation | async-start | bytes 2162688 | tf_op jit(solution)/shard_map/all_gather | solution.py:63
  7.7 9.3 %collective-permute-start = (f32[32,1,128]{2,0,1:T(8,128)S(1)}, f32[32,1,128]{2,0,1:T(8,128)S(1)}, u32[]{:S(2)}, u32[]{:S(2)}) collective-permute-start(f32[32,1,128]{2,0,1:T(8,128)S(1)} %bitcast.50), channel_id=1, source_target_pairs={{8,0},{16,8},{24,16},{32,24},{40,32},{48,40},{56,48},{64,56},{72,6... | collective-permute-start | bytes 49160 | tf_op jit(solution)/shard_map/ppermute | solution.py:17
  15.5 6.8 %collective-permute-start.1 = (f32[32,1,128]{2,0,1:T(8,128)S(1)}, f32[32,1,128]{2,0,1:T(8,128)S(1)}, u32[]{:S(2)}, u32[]{:S(2)}) collective-permute-start(f32[32,1,128]{2,0,1:T(8,128)S(1)} %bitcast.49), channel_id=1, source_target_pairs={{0,8},{8,16},{16,24},{24,32},{32,40},{40,48},{48,56},{56,64},{64,7... | collective-permute-start | bytes 49160 | tf_op jit(solution)/shard_map/ppermute | solution.py:16
  26.7 5.9 %collective-permute-start.2 = (f32[32,66,1]{1,0,2:T(8,128)S(1)}, f32[32,66,1]{1,0,2:T(8,128)S(1)}, u32[]{:S(2)}, u32[]{:S(2)}) collective-permute-start(f32[32,66,1]{1,0,2:T(8,128)S(1)} %copy.61), channel_id=1, source_target_pairs={{1,0},{2,1},{3,2},{4,3},{5,4},{6,5},{7,6},{0,7},{9,8},{10,9},{11,1... | collective-permute-start | bytes 25352 | tf_op jit(solution)/shard_map/ppermute | solution.py:17
  28.0 6.2 %collective-permute-start.3 = (f32[32,66,1]{1,0,2:T(8,128)S(1)}, f32[32,66,1]{1,0,2:T(8,128)S(1)}, u32[]{:S(2)}, u32[]{:S(2)}) collective-permute-start(f32[32,66,1]{1,0,2:T(8,128)S(1)} %copy.63), channel_id=1, source_target_pairs={{0,1},{1,2},{2,3},{3,4},{4,5},{5,6},{6,7},{7,0},{8,9},{9,10},{10,1... | collective-permute-start | bytes 25352 | tf_op jit(solution)/shard_map/ppermute | solution.py:16
  41.0 7.5 %copy-start.1 = (f32[1,32,64,128]{3,2,1,0:T(8,128)}, f32[1,32,64,128]{3,2,1,0:T(8,128)S(1)}, u32[]{:S(2)}) copy-start(f32[1,32,64,128]{3,2,1,0:T(8,128)S(1)} %get-tuple-element.22) | copy-start | bytes 3145732
  41.1 7.0 %collective-permute-start.4 = (f32[2,32,1,128]{3,1,2,0:T(8,128)S(1)}, f32[2,32,1,128]{3,1,2,0:T(8,128)S(1)}, u32[]{:S(2)}, u32[]{:S(2)}) collective-permute-start(f32[2,32,1,128]{3,1,2,0:T(8,128)S(1)} %bitcast.48), channel_id=1, source_target_pairs={{0,8},{8,16},{16,24},{24,32},{32,40},{40,48},{48,56},{56,64},{64,7... | collective-permute-start | bytes 98312 | tf_op jit(solution)/shard_map/ppermute | solution.py:16
  41.2 6.9 %collective-permute-start.5 = (f32[2,32,1,128]{3,1,2,0:T(8,128)S(1)}, f32[2,32,1,128]{3,1,2,0:T(8,128)S(1)}, u32[]{:S(2)}, u32[]{:S(2)}) collective-permute-start(f32[2,32,1,128]{3,1,2,0:T(8,128)S(1)} %bitcast.47), channel_id=1, source_target_pairs={{8,0},{16,8},{24,16},{32,24},{40,32},{48,40},{56,48},{64,56},{72,6... | collective-permute-start | bytes 98312 | tf_op jit(solution)/shard_map/ppermute | solution.py:17
  53.8 5.9 %collective-permute-start.6 = (f32[2,32,66,1]{2,1,3,0:T(8,128)S(1)}, f32[2,32,66,1]{2,1,3,0:T(8,128)S(1)}, u32[]{:S(2)}, u32[]{:S(2)}) collective-permute-start(f32[2,32,66,1]{2,1,3,0:T(8,128)S(1)} %copy.69), channel_id=1, source_target_pairs={{0,1},{1,2},{2,3},{3,4},{4,5},{5,6},{6,7},{7,0},{8,9},{9,10},{10,1... | collective-permute-start | bytes 50696 | tf_op jit(solution)/shard_map/ppermute | solution.py:16
  59.4 6.3 %collective-permute-start.7 = (f32[2,32,66,1]{2,1,3,0:T(8,128)S(1)}, f32[2,32,66,1]{2,1,3,0:T(8,128)S(1)}, u32[]{:S(2)}, u32[]{:S(2)}) collective-permute-start(f32[2,32,66,1]{2,1,3,0:T(8,128)S(1)} %copy.70), channel_id=1, source_target_pairs={{1,0},{2,1},{3,2},{4,3},{5,4},{6,5},{7,6},{0,7},{9,8},{10,9},{11,1... | collective-permute-start | bytes 50696 | tf_op jit(solution)/shard_map/ppermute | solution.py:17
  73.2 1.2 copy-start.2
  74.4 7.1 %copy-start.6 = (s32[4]{0:T(128)S(1)}, s32[4]{0:T(128)}, u32[]{:S(2)}) copy-start(s32[4]{0:T(128)} %constant.74.clone) | copy-start | bytes 52
  79.7 83.7 %copy-start.3 = (f32[32,64,128]{2,1,0:T(8,128)S(1)}, f32[32,64,128]{2,1,0:T(8,128)}, u32[]{:S(2)}) copy-start(f32[32,64,128]{2,1,0:T(8,128)} %convolution_bitcast_fusion.1) | copy-start | bytes 3145732
  79.7 83.7 %copy-start.4 = (f32[32,64,4]{1,2,0:T(4,128)S(1)}, f32[32,64,4]{1,2,0:T(4,128)}, u32[]{:S(2)}) copy-start(f32[32,64,4]{1,2,0:T(4,128)} %param.13) | copy-start | bytes 98308
  171.2 33.5 %copy-start.5 = (f32[32,128,4]{1,2,0:T(4,128)S(1)}, f32[32,128,4]{1,2,0:T(4,128)}, u32[]{:S(2)}) copy-start(f32[32,128,4]{1,2,0:T(4,128)} %param.16) | copy-start | bytes 196612
Sparse Core Ops, SparseCore 0:
  81.7 77.3 all-gather.1
where the time goes:
time: 215 us; the launch traced here: 214 us
  waiting for transfers between devices  87.5 us (41%)
  local copies, waits for them, and re-layouts  31.3 us (15%)
  blocking collectives  29.4 us (14%)
  starting transfers between devices  20.9 us (10%)
  matrix products  19.3 us (9%)
  between operations  13.6 us (6%)
  other arithmetic  12.3 us (6%)
    all_gather x1, waiting for transfers between devices, solve_x(): gathered = lax.all_gather(rims, 'gx', axis=1, tiled=True)  74.2 us
    all_gather x1, blocking collectives, solve_y(): gathered = lax.all_gather(rims, 'gy', axis=1, tiled=True)  29.4 us
    ppermute x4, starting transfers between devices, extended_2(): after = lax.ppermute(leading, axis, down)  14.2 us
    ppermute x4, waiting for transfers between devices, extended_2(): before = lax.ppermute(last, axis, up)  6.93 us
    slice x4, local copies, waits for them, and re-layouts, extended_2(): last = lax.slice_in_dim(shard, length - width, length, axis=dim)  6.9 us
    concatenate x3, other arithmetic, extended_2(): shard = jnp.concatenate([before, shard, after], axis=dim)  6.88 us
    ppermute x4, starting transfers between devices, extended_2(): before = lax.ppermute(last, axis, up)  6.69 us
    ppermute x4, waiting for transfers between devices, extended_2(): after = lax.ppermute(leading, axis, down)  6.4 us
  transfers between devices with their start and end apart: 9, of which 6 were waited for; matrix products, arithmetic and copies ran while one was open for 5% of the time, Pallas kernels for 0%

commit v1 on v0

--- a/solution.py
+++ b/solution.py
@@ -74,7 +74,9 @@
     rims = jnp.transpose(
         jnp.concatenate([lin[:, :, 0:2], lin[:, :, width - 2 :]], axis=2), (0, 2, 1)
     )
-    gathered = lax.all_gather(rims, "gy", axis=1, tiled=True)
+    gathered = jnp.concatenate(
+        lax.all_to_all(jnp.stack([rims] * lax.axis_size("gy")), "gy", 0, 0), axis=1
+    )
     whole = reduced_y.shape[1]
     place = lax.axis_index("gy")
     offsets = jnp.array([-2, -1, 4, 5], jnp.int32)

time: 215 us -> 206 us (0.958)
  blocking collectives: 29.4 us -> 0 us
  local copies, waits for them, and re-layouts: 31.3 us -> 36.6 us
  waiting for transfers between devices: 87.5 us -> 92.7 us
  starting transfers between devices: 20.9 us -> 25.7 us
  other arithmetic: 12.3 us -> 14.6 us
    all_gather x1 -> x0, blocking collectives: 29.4 us -> none  [solve_y(): gathered = lax.all_gather(rims, 'gy', axis=1, tiled=True)]
    unnamed x14 -> x19, local copies, waits for them, and re-layouts: 0.92 us -> 5.76 us
    all_to_all x0 -> x1, starting transfers between devices: none -> 4.79 us  [solve_y(): lax.all_to_all(jnp.stack([rims] * lax.axis_size('gy')), 'gy', 0, 0)]
    all_to_all x0 -> x1, waiting for transfers between devices: none -> 3.49 us  [solve_y(): lax.all_to_all(jnp.stack([rims] * lax.axis_size('gy')), 'gy', 0, 0)]
    all_to_all x0 -> x1, other arithmetic: none -> 2.24 us  [solve_y(): lax.all_to_all(jnp.stack([rims] * lax.axis_size('gy')), 'gy', 0, 0)]
  transfers between devices with their start and end apart: 9 -> 10, of which waited for: 6 -> 7; matrix products, arithmetic and copies ran while one was open for 5% -> 5% of each run, Pallas kernels for 0% -> 0%
where the time goes in v1:
time: 206 us; the launch traced here: 204 us
  waiting for transfers between devices  92.7 us (45%)
  local copies, waits for them, and re-layouts  36.6 us (18%)
  starting transfers between devices  25.7 us (12%)
  matrix products  20.3 us (10%)
  other arithmetic  14.6 us (7%)
  between operations  13.6 us (7%)
    all_gather x1, waiting for transfers between devices, solve_x(): gathered = lax.all_gather(rims, 'gx', axis=1, tiled=True)  75.9 us
    ppermute x4, starting transfers between devices, extended_2(): after = lax.ppermute(leading, axis, down)  14.2 us
    ppermute x4, waiting for transfers between devices, extended_2(): before = lax.ppermute(last, axis, up)  6.93 us
    slice x4, local copies, waits for them, and re-layouts, extended_2(): last = lax.slice_in_dim(shard, length - width, length, axis=dim)  6.89 us
    concatenate x3, other arithmetic, extended_2(): shard = jnp.concatenate([before, shard, after], axis=dim)  6.88 us
    ppermute x4, starting transfers between devices, extended_2(): before = lax.ppermute(last, axis, up)  6.69 us
    ppermute x4, waiting for transfers between devices, extended_2(): after = lax.ppermute(leading, axis, down)  6.4 us
    unnamed x19, local copies, waits for them, and re-layouts  5.76 us
  transfers between devices with their start and end apart: 10, of which 7 were waited for; matrix products, arithmetic and copies ran while one was open for 5% of the time, Pallas kernels for 0%

profile of v1, /device:TPU:24, one launch (start us, length us, event | category | flops | bytes accessed | tf_op | source)
XLA Modules:
  0.0 203.5 jit_solution(1381720471441324296)
XLA Ops:
  7.7 7.8 %collective-permute-start = (f32[32,1,128]{2,0,1:T(8,128)S(1)}, f32[32,1,128]{2,0,1:T(8,128)S(1)}, u32[]{:S(2)}, u32[]{:S(2)}) collective-permute-start(f32[32,1,128]{2,0,1:T(8,128)S(1)} %bitcast.57), channel_id=1, source_target_pairs={{8,0},{16,8},{24,16},{32,24},{40,32},{48,40},{56,48},{64,56},{72,6... | collective-permute-start | bytes 49160 | tf_op jit(solution)/shard_map/ppermute | solution.py:17
  17.0 5.3 %collective-permute-done.1 = f32[32,1,128]{2,0,1:T(8,128)S(1)} collective-permute-done((f32[32,1,128]{2,0,1:T(8,128)S(1)}, f32[32,1,128]{2,0,1:T(8,128)S(1)}, u32[]{:S(2)}, u32[]{:S(2)}) %collective-permute-start.1) | collective-permute-done | bytes 16416 | tf_op jit(solution)/shard_map/ppermute | solution.py:16
  25.0 1.7 copy.63
  28.0 3.4 %collective-permute-start.3 = (f32[32,66,1]{1,0,2:T(8,128)S(1)}, f32[32,66,1]{1,0,2:T(8,128)S(1)}, u32[]{:S(2)}, u32[]{:S(2)}) collective-permute-start(f32[32,66,1]{1,0,2:T(8,128)S(1)} %copy.65), channel_id=1, source_target_pairs={{0,1},{1,2},{2,3},{3,4},{4,5},{5,6},{6,7},{7,0},{8,9},{9,10},{10,1... | collective-permute-start | bytes 25352 | tf_op jit(solution)/shard_map/ppermute | solution.py:16
  34.2 1.5 copy.66
  35.7 5.3 %fusion.7 = (f32[1,32,64,128]{3,2,1,0:T(8,128)S(1)}, f32[1,32,64,128]{3,2,1,0:T(8,128)S(1)}) fusion(f32[32,64,128]{2,1,0:T(8,128)} %param.10, f32[32,66,1]{2,1,0:T(8,128)} %copy.66, f32[32,1,128]{2,1,0:T(1,128)S(1)} %bitcast.51, f32[32,1,128]{2,1,0:T(1,128)S(1)} %bitcast.53, f32[32,66,1]{2,1,0:T(8,128)} %copy.64, f32[32,64,128]{2,1,0:T(8,128)} %param.11), kind=kLoop, calls=%fused_computation.20 | loop fusion | flops 5505024 | bytes 4243968 | tf_op jit(solution)/shard_map/stack | solution.py:93
  41.2 5.3 %collective-permute-start.5 = (f32[2,32,1,128]{3,1,2,0:T(8,128)S(1)}, f32[2,32,1,128]{3,1,2,0:T(8,128)S(1)}, u32[]{:S(2)}, u32[]{:S(2)}) collective-permute-start(f32[2,32,1,128]{3,1,2,0:T(8,128)S(1)} %bitcast.54), channel_id=1, source_target_pairs={{8,0},{16,8},{24,16},{32,24},{40,32},{48,40},{56,48},{64,56},{72,6... | collective-permute-start | bytes 98312 | tf_op jit(solution)/shard_map/ppermute | solution.py:17
  46.5 1.6 collective-permute-done.4
  48.5 2.9 %fusion.53 = (f32[2,32,66,1]{3,2,1,0:T(8,128)}, f32[2,32,66,1]{3,2,1,0:T(8,128)}) fusion(f32[2,32,66,128]{3,2,1,0:T(8,128)S(1)} %pad_maximum_fusion.1), kind=kLoop, calls=%fused_computation.90 | loop fusion | bytes 67584 | tf_op jit(solution)/shard_map/slice | solution.py:14
  51.3 2.4 %copy.71 = f32[2,32,66,1]{2,1,3,0:T(8,128)S(1)} copy(f32[2,32,66,1]{3,2,1,0:T(8,128)} %get-tuple-element.11) | data formatting | bytes 33792 | tf_op jit(solution)/shard_map/slice | solution.py:14
  53.8 3.2 %collective-permute-start.6 = (f32[2,32,66,1]{2,1,3,0:T(8,128)S(1)}, f32[2,32,66,1]{2,1,3,0:T(8,128)S(1)}, u32[]{:S(2)}, u32[]{:S(2)}) collective-permute-start(f32[2,32,66,1]{2,1,3,0:T(8,128)S(1)} %copy.71), channel_id=1, source_target_pairs={{0,1},{1,2},{2,3},{3,4},{4,5},{5,6},{6,7},{7,0},{8,9},{9,10},{10,1... | collective-permute-start | bytes 50696 | tf_op jit(solution)/shard_map/ppermute | solution.py:16
  57.0 2.4 %copy.72 = f32[2,32,66,1]{2,1,3,0:T(8,128)S(1)} copy(f32[2,32,66,1]{3,2,1,0:T(8,128)} %get-tuple-element.12) | data formatting | bytes 33792 | tf_op jit(solution)/shard_map/slice | solution.py:15
  59.7 2.3 %copy.73 = f32[2,32,66,1]{3,2,1,0:T(8,128)} copy(f32[2,32,66,1]{2,1,3,0:T(8,128)S(1)} %collective-permute-done.6) | data formatting | bytes 33792 | tf_op jit(solution)/shard_map/ppermute | solution.py:16
  61.9 3.7 %collective-permute-done.7 = f32[2,32,66,1]{2,1,3,0:T(8,128)S(1)} collective-permute-done((f32[2,32,66,1]{2,1,3,0:T(8,128)S(1)}, f32[2,32,66,1]{2,1,3,0:T(8,128)S(1)}, u32[]{:S(2)}, u32[]{:S(2)}) %collective-permute-start.7) | collective-permute-done | bytes 16928 | tf_op jit(solution)/shard_map/ppermute | solution.py:17
  65.7 2.3 %copy.74 = f32[2,32,66,1]{3,2,1,0:T(8,128)} copy(f32[2,32,66,1]{2,1,3,0:T(8,128)S(1)} %collective-permute-done.7) | data formatting | bytes 33792 | tf_op jit(solution)/shard_map/ppermute | solution.py:17
  68.0 5.2 %pad_maximum_fusion = f32[2,32,66,130]{3,2,1,0:T(8,128)S(1)} fusion(f32[2,32,66,1]{3,2,1,0:T(8,128)} %copy.74, f32[2,32,1,128]{3,2,1,0:T(1,128)S(1)} %bitcast.49, f32[1,32,64,128]{3,2,1,0:T(8,128)} %copy-done.1, f32[1,32,64,128]{3,2,1,0:T(8,128)S(1)} %get-tuple-element.21, f32[2,32,1,128]{3,2,1,0:T(1,128)S(1)} %bitcast.47, f32[2,32,66,1]{3,2,1,0:T(8,128)} %copy.73), kind=kLoop, calls=%fused_computation.2 | loop fusion | flops 2745600 | bytes 4392960 | tf_op jit(solution)/shard_map/concatenate | solution.py:18
  74.4 5.3 %convolution_bitcast_fusion.1 = f32[32,64,128]{2,1,0:T(8,128)} fusion(f32[32,64,64]{2,1,0:T(8,128)} %param.12, f32[32,64,128]{2,1,0:T(8,128)S(1)} %copy-done.2, f32[32,66,130]{2,1,0:T(8,128)S(1)} %get-tuple-element.10, f32[32,66,130]{2,1,0:T(8,128)S(1)} %get-tuple-element.9), kind=kOutput, calls=%fused_computation.14 | convolution fusion | flops 206831616 | bytes 13107200 | tf_op jit(solution)/shard_map/zij,zjn->zin/dot_general | solution.py:59
  81.6 1.6 gather_fusion
  83.1 75.9 %all-gather.2.cloned.1.call-done = f32[32,128,128]{2,0,1:T(8,128)} async-done(((f32[32,4,128]{2,0,1:T(8,128)}), f32[32,128,128]{2,0,1:T(8,128)}) %all-gather.2.cloned.1.call-update) | async-done | bytes 2097168 | tf_op jit(solution)/shard_map/all_gather | solution.py:63
  159.0 4.4 %fusion = f32[32,4,128]{2,1,0:T(4,128)S(1)} fusion(f32[32,128,128]{2,0,1:T(8,128)} %all-gather.2.cloned.1.call-done, f32[4,32,128]{2,0,1:T(4,128)S(1)} %gather_fusion, pred[4]{0:T(512)(128)(4,1)S(1)} %get-tuple-element.25), kind=kOutput, calls=%fused_computation.6 | convolution fusion | flops 25182208 | bytes 2228228 | tf_op jit(solution)/shard_map/zrk,zkn->zrn/dot_general | solution.py:67
  163.4 1.8 fusion.2
  165.3 4.1 %fusion.58 = f32[32,64,128]{2,1,0:T(8,128)S(1)} fusion(f32[32,64,128]{2,1,0:T(8,128)S(1)} %fusion.2, f32[32,128,128]{2,1,0:T(8,128)S(1)} %copy-done), kind=kOutput, calls=%fused_computation.96 | convolution fusion | flops 402653184 | bytes 4194304 | tf_op jit(solution)/shard_map/zij,zxj->zxi/dot_general | solution.py:73
  169.4 1.7 fusion.55
  171.1 1.6 copy.77
  172.7 1.6 copy.78
  175.2 2.3 %reshape.38 = f32[8,1,8192]{2,1,0:T(1,128)} reshape(f32[8,4,32,64]{3,2,1,0:T(8,128)} %broadcast_bitcast_fusion) | data formatting | bytes 524288
  177.5 4.8 %all-to-all-start = ((f32[8,1,8192]{2,1,0:T(1,128)}), f32[8,1,8192]{2,1,0:T(1,128)S(1)}, u32[]{:S(2)}, u32[]{:S(2)}) async-start(f32[8,1,8192]{2,1,0:T(1,128)} %reshape.38), calls=%async_computation | async-start | bytes 524288 | tf_op jit(solution)/shard_map/all_to_all | solution.py:78
  182.3 1.7 gather_fusion.1
  184.0 3.5 %all-to-all-done = f32[8,1,8192]{2,1,0:T(1,128)S(1)} async-done(((f32[8,1,8192]{2,1,0:T(1,128)}), f32[8,1,8192]{2,1,0:T(1,128)S(1)}, u32[]{:S(2)}, u32[]{:S(2)}) %all-to-all-start) | async-done | bytes 262176 | tf_op jit(solution)/shard_map/all_to_all | solution.py:78
  188.8 2.2 %reduce = f32[8,8192]{1,0:T(8,128)S(1)} reduce(f32[8,1,8192]{2,1,0:T(1,128)} %copy-done.4, f32[]{:T(128)} %broadcast.78), dimensions={1}, to_apply=%all_to_all.3.reduce_sub_computation | reduce | bytes 524292 | tf_op jit(solution)/shard_map/all_to_all | solution.py:78
  192.0 1.8 fusion.35
  193.9 2.8 %convolution_subtract_fusion = f32[32,64,128]{2,1,0:T(8,128)} fusion(f32[32,64,128]{2,1,0:T(8,128)S(1)} %fusion.58, f32[32,4,64]{2,1,0:T(4,128)S(1)} %fusion.35, f32[32,128,4]{1,2,0:T(4,128)S(1)} %copy-done.6), kind=kOutput, calls=%fused_computation.11 | convolution fusion | flops 12845056 | bytes 2195456 | tf_op jit(solution)/shard_map/zik,zkx->zxi/dot_general | solution.py:86
  (45 shorter events, 16.2 us)
Async XLA Ops:
  6.5 158.7 %copy-start = (f32[32,128,128]{2,1,0:T(8,128)S(1)}, f32[32,128,128]{2,1,0:T(8,128)}, u32[]{:S(2)}) copy-start(f32[32,128,128]{2,1,0:T(8,128)} %param.15) | copy-start | bytes 6291460
  6.5 152.5 %all-gather.2.cloned.1.call-start = ((), (), s32[]{:S(2)}) async-start(), calls=%async_computation.1 | async-start | bytes 2162688 | tf_op jit(solution)/shard_map/all_gather | solution.py:63
  7.7 9.3 %collective-permute-start = (f32[32,1,128]{2,0,1:T(8,128)S(1)}, f32[32,1,128]{2,0,1:T(8,128)S(1)}, u32[]{:S(2)}, u32[]{:S(2)}) collective-permute-start(f32[32,1,128]{2,0,1:T(8,128)S(1)} %bitcast.57), channel_id=1, source_target_pairs={{8,0},{16,8},{24,16},{32,24},{40,32},{48,40},{56,48},{64,56},{72,6... | collective-permute-start | bytes 49160 | tf_op jit(solution)/shard_map/ppermute | solution.py:17
  15.5 6.8 %collective-permute-start.1 = (f32[32,1,128]{2,0,1:T(8,128)S(1)}, f32[32,1,128]{2,0,1:T(8,128)S(1)}, u32[]{:S(2)}, u32[]{:S(2)}) collective-permute-start(f32[32,1,128]{2,0,1:T(8,128)S(1)} %bitcast.56), channel_id=1, source_target_pairs={{0,8},{8,16},{16,24},{24,32},{32,40},{40,48},{48,56},{56,64},{64,7... | collective-permute-start | bytes 49160 | tf_op jit(solution)/shard_map/ppermute | solution.py:16
  26.7 5.9 %collective-permute-start.2 = (f32[32,66,1]{1,0,2:T(8,128)S(1)}, f32[32,66,1]{1,0,2:T(8,128)S(1)}, u32[]{:S(2)}, u32[]{:S(2)}) collective-permute-start(f32[32,66,1]{1,0,2:T(8,128)S(1)} %copy.63), channel_id=1, source_target_pairs={{1,0},{2,1},{3,2},{4,3},{5,4},{6,5},{7,6},{0,7},{9,8},{10,9},{11,1... | collective-permute-start | bytes 25352 | tf_op jit(solution)/shard_map/ppermute | solution.py:17
  28.0 6.2 %collective-permute-start.3 = (f32[32,66,1]{1,0,2:T(8,128)S(1)}, f32[32,66,1]{1,0,2:T(8,128)S(1)}, u32[]{:S(2)}, u32[]{:S(2)}) collective-permute-start(f32[32,66,1]{1,0,2:T(8,128)S(1)} %copy.65), channel_id=1, source_target_pairs={{0,1},{1,2},{2,3},{3,4},{4,5},{5,6},{6,7},{7,0},{8,9},{9,10},{10,1... | collective-permute-start | bytes 25352 | tf_op jit(solution)/shard_map/ppermute | solution.py:16
  41.0 7.5 %copy-start.1 = (f32[1,32,64,128]{3,2,1,0:T(8,128)}, f32[1,32,64,128]{3,2,1,0:T(8,128)S(1)}, u32[]{:S(2)}) copy-start(f32[1,32,64,128]{3,2,1,0:T(8,128)S(1)} %get-tuple-element.22) | copy-start | bytes 3145732
  41.1 7.0 %collective-permute-start.4 = (f32[2,32,1,128]{3,1,2,0:T(8,128)S(1)}, f32[2,32,1,128]{3,1,2,0:T(8,128)S(1)}, u32[]{:S(2)}, u32[]{:S(2)}) collective-permute-start(f32[2,32,1,128]{3,1,2,0:T(8,128)S(1)} %bitcast.55), channel_id=1, source_target_pairs={{0,8},{8,16},{16,24},{24,32},{32,40},{40,48},{48,56},{56,64},{64,7... | collective-permute-start | bytes 98312 | tf_op jit(solution)/shard_map/ppermute | solution.py:16
  41.2 6.9 %collective-permute-start.5 = (f32[2,32,1,128]{3,1,2,0:T(8,128)S(1)}, f32[2,32,1,128]{3,1,2,0:T(8,128)S(1)}, u32[]{:S(2)}, u32[]{:S(2)}) collective-permute-start(f32[2,32,1,128]{3,1,2,0:T(8,128)S(1)} %bitcast.54), channel_id=1, source_target_pairs={{8,0},{16,8},{24,16},{32,24},{40,32},{48,40},{56,48},{64,56},{72,6... | collective-permute-start | bytes 98312 | tf_op jit(solution)/shard_map/ppermute | solution.py:17
  53.8 5.9 %collective-permute-start.6 = (f32[2,32,66,1]{2,1,3,0:T(8,128)S(1)}, f32[2,32,66,1]{2,1,3,0:T(8,128)S(1)}, u32[]{:S(2)}, u32[]{:S(2)}) collective-permute-start(f32[2,32,66,1]{2,1,3,0:T(8,128)S(1)} %copy.71), channel_id=1, source_target_pairs={{0,1},{1,2},{2,3},{3,4},{4,5},{5,6},{6,7},{7,0},{8,9},{9,10},{10,1... | collective-permute-start | bytes 50696 | tf_op jit(solution)/shard_map/ppermute | solution.py:16
  59.4 6.3 %collective-permute-start.7 = (f32[2,32,66,1]{2,1,3,0:T(8,128)S(1)}, f32[2,32,66,1]{2,1,3,0:T(8,128)S(1)}, u32[]{:S(2)}, u32[]{:S(2)}) collective-permute-start(f32[2,32,66,1]{2,1,3,0:T(8,128)S(1)} %copy.72), channel_id=1, source_target_pairs={{1,0},{2,1},{3,2},{4,3},{5,4},{6,5},{7,6},{0,7},{9,8},{10,9},{11,1... | collective-permute-start | bytes 50696 | tf_op jit(solution)/shard_map/ppermute | solution.py:17
  73.2 1.2 copy-start.2
  74.4 7.1 %copy-start.7 = (s32[4]{0:T(128)S(1)}, s32[4]{0:T(128)}, u32[]{:S(2)}) copy-start(s32[4]{0:T(128)} %constant.74.clone) | copy-start | bytes 52
  79.7 83.7 %copy-start.3 = (f32[32,64,128]{2,1,0:T(8,128)S(1)}, f32[32,64,128]{2,1,0:T(8,128)}, u32[]{:S(2)}) copy-start(f32[32,64,128]{2,1,0:T(8,128)} %convolution_bitcast_fusion.1) | copy-start | bytes 3145732
  79.7 83.7 %copy-start.5 = (f32[32,64,4]{1,2,0:T(4,128)S(1)}, f32[32,64,4]{1,2,0:T(4,128)}, u32[]{:S(2)}) copy-start(f32[32,64,4]{1,2,0:T(4,128)} %param.13) | copy-start | bytes 98308
  174.3 19.5 %copy-start.6 = (f32[32,128,4]{1,2,0:T(4,128)S(1)}, f32[32,128,4]{1,2,0:T(4,128)}, u32[]{:S(2)}) copy-start(f32[32,128,4]{1,2,0:T(4,128)} %param.16) | copy-start | bytes 196612
  177.5 10.0 %all-to-all-start = ((f32[8,1,8192]{2,1,0:T(1,128)}), f32[8,1,8192]{2,1,0:T(1,128)S(1)}, u32[]{:S(2)}, u32[]{:S(2)}) async-start(f32[8,1,8192]{2,1,0:T(1,128)} %reshape.38), calls=%async_computation | async-start | bytes 524288 | tf_op jit(solution)/shard_map/all_to_all | solution.py:78
  187.5 0.7 copy-start.4
Sparse Core Ops, SparseCore 0:
  81.6 77.3 all-gather.1
